TPU v7x, 32 devices: a whole 2x2x4 slice. The times are simulated.
32 devices in a mesh: grp: 4 (over y, x), seq: 8 (over z, core).
Axes of the slice: x: 2, y: 2, z: 4, core: 2. Of those that a mesh axis runs over, the one named last changes fastest.
Arguments:
- owned_patches: bfloat16 [4, 1024, 1152], P('grp', 'seq'), may hold values from -6 to 6
- send_rows: int32 [4, 8, 128], P('grp', 'seq'), may hold values from 0 to 127, each once within a row
- receive_slot: int32 [4, 8, 128], P('grp', 'seq'), may hold values from 0 to 127, each once within a row
- segment_ids: int32 [4, 1024], P('grp', 'seq'), may hold values from 0 to 15, never falling along the last dimension, each value on 1 to 640 neighbouring positions
- class_label: int32 [4, 16], P('grp'), may hold values from 0 to 999
- drop_mask: int32 [4, 16], P('grp'), may hold values 0 or 1
- class_table: bfloat16 [1001, 1152], replicated, may hold values from -6 to 6
- modulation_weight: bfloat16 [1152, 3456], replicated, may hold values from -0.1875 to 0.1875
- attention_in: bfloat16 [1152, 1728], replicated, may hold values from -0.1875 to 0.1875
- attention_out: bfloat16 [576, 1152], replicated, may hold values from -0.25 to 0.25
- cotangent: bfloat16 [4, 1024, 1152], P('grp', 'seq'), may hold values from -6 to 6
Outputs:
- layer_output: bfloat16 [4, 1024, 1152], P('grp', 'seq')
- owner_gradient: bfloat16 [4, 1024, 1152], P('grp', 'seq')
- gradient_in: bfloat16 [1152, 1728], replicated
- gradient_out: bfloat16 [576, 1152], replicated
Inputs may be any that keep to these rules, and one draw needn't show every extreme that they name: `send_rows`: for owner shard s of a group, entries 16 * d to 16 * d + 15 name, in slot order, the local rows that go to packed shard d; every local row once. `receive_slot`: packed row r of packed shard d takes slot c of what owner shard s sends to d, where the entry is 16 * s + c; every slot once. `segment_ids`: never falling along a group's tokens; every image has 1 to 640 tokens, one exactly 640.
All inputs are finite; a program needn't handle non-finite values. No bound on the sum of `drop_mask` on one device may be relied on, other than what follows from the above.
Results may differ from a plain program's by a relative error of at most 0.015.
Values may be sent and summed in bfloat16 or wider, within the bound.
A program may use at most 128 MiB of HBM per device.

v0:
```python
import math
import jax
import jax.numpy as jnp
from jax import lax
from jax.sharding import PartitionSpec as P

HEADS = 8
CLASSES = 1000
EPSILON = 1e-06


def normalize(values):
    center = values - jnp.mean(values, axis=-1, keepdims=True)
    spread = jnp.mean(center * center, axis=-1, keepdims=True)
    inverse_spread = lax.rsqrt(spread + EPSILON)
    return (center * inverse_spread, inverse_spread)


def exponent(query_heads, key_heads, image_query, image_keys, factor):
    logits = (
        jnp.einsum("qhe,khe->qhk", query_heads, key_heads, preferred_element_type=jnp.float32)
        * factor
    )
    joined = (image_query[:, None] == image_keys[None, :])[:, None, :]
    return jnp.exp(jnp.where(joined, logits, -jnp.inf))


def shards(
    owned_patches,
    send_rows,
    receive_slot,
    segment_ids,
    class_label,
    drop_mask,
    class_table,
    modulation_weight,
    attention_in,
    attention_out,
    cotangent,
):
    shard_count = lax.axis_size("seq")
    tokens = owned_patches.shape[1]
    model_width = owned_patches.shape[2]
    inner_width = attention_out.shape[0]
    head_width = inner_width // HEADS
    factor = head_width ** (-0.5)
    outgoing = jnp.take(owned_patches[0], send_rows[0, 0], axis=0)
    incoming = lax.all_to_all(outgoing, "seq", split_axis=0, concat_axis=0, tiled=True)
    packed = jnp.take(incoming, receive_slot[0, 0], axis=0)
    chosen = jnp.where(drop_mask[0] == 1, CLASSES, class_label[0])
    condition = jnp.take(class_table, chosen, axis=0)
    activated = jax.nn.silu(condition.astype(jnp.float32)).astype(jnp.bfloat16)
    modulation = jnp.dot(activated, modulation_weight, preferred_element_type=jnp.float32)
    local_images = segment_ids[0]
    image_count = class_label.shape[1]
    one_hot = (local_images[:, None] == jnp.arange(image_count, dtype=jnp.int32)[None, :]).astype(
        jnp.float32
    )
    per_token = jnp.dot(
        one_hot, modulation, precision=lax.Precision.HIGHEST, preferred_element_type=jnp.float32
    )
    shift_rows = per_token[:, :model_width]
    scale_rows = per_token[:, model_width : 2 * model_width]
    gate_rows = per_token[:, 2 * model_width :]
    row_values = packed.astype(jnp.float32)
    normed, inverse_spread = normalize(row_values)
    hidden = (normed * (1.0 + scale_rows) + shift_rows).astype(jnp.bfloat16)
    projected_in = jnp.dot(hidden, attention_in, preferred_element_type=jnp.float32).astype(
        jnp.bfloat16
    )
    queries = projected_in[:, :inner_width]
    key_value = projected_in[:, inner_width:]
    all_key_value, all_images = (
        lax.all_gather(key_value, "seq", axis=0, tiled=True),
        lax.all_gather(local_images, "seq", axis=0, tiled=True),
    )
    total_rows = all_key_value.shape[0]
    block_rows = math.gcd(total_rows, 512)
    block_count = total_rows // block_rows
    query_heads = queries.reshape(tokens, HEADS, head_width)

    def key_block(block_index):
        first_row = block_index * block_rows
        block_pair = lax.dynamic_slice_in_dim(all_key_value, first_row, block_rows, 0)
        block_images = lax.dynamic_slice_in_dim(all_images, first_row, block_rows, 0)
        key_heads = block_pair[:, :inner_width].reshape(block_rows, HEADS, head_width)
        value_heads = block_pair[:, inner_width:].reshape(block_rows, HEADS, head_width)
        return (key_heads, value_heads, block_images)

    def forward_step(block_index, carried):
        weighted, totals = carried
        key_heads, value_heads, block_images = key_block(block_index)
        powers = exponent(query_heads, key_heads, local_images, block_images, factor)
        totals = totals + jnp.sum(powers, axis=-1)
        weighted = weighted + jnp.einsum(
            "qhk,khe->qhe",
            powers.astype(jnp.bfloat16),
            value_heads,
            preferred_element_type=jnp.float32,
        )
        return (weighted, totals)

    start_state = (
        jnp.zeros((tokens, HEADS, head_width), jnp.float32),
        jnp.zeros((tokens, HEADS), jnp.float32),
    )
    weighted, totals = lax.fori_loop(0, block_count, forward_step, start_state)
    attended = (weighted / totals[:, :, None]).reshape(tokens, inner_width).astype(jnp.bfloat16)
    projected = jnp.dot(attended, attention_out, preferred_element_type=jnp.float32)
    layer_output = (row_values + gate_rows * projected).astype(jnp.bfloat16)
    contract_rows = (((0,), (0,)), ((), ()))
    contract_last = (((1,), (1,)), ((), ()))
    upstream = cotangent[0].astype(jnp.float32)
    branch = (gate_rows * upstream).astype(jnp.bfloat16)
    out_weight_term = lax.dot_general(
        attended, branch, contract_rows, preferred_element_type=jnp.float32
    )
    attended_cotangent = lax.dot_general(
        branch, attention_out, contract_last, preferred_element_type=jnp.float32
    ).astype(jnp.bfloat16)
    cotangent_heads = attended_cotangent.reshape(tokens, HEADS, head_width)
    attended_heads = attended.reshape(tokens, HEADS, head_width)
    delta_rows = jnp.sum(
        cotangent_heads.astype(jnp.float32) * attended_heads.astype(jnp.float32), axis=-1
    )

    def query_step(block_index, carried):
        key_heads, value_heads, block_images = key_block(block_index)
        weights = (
            exponent(query_heads, key_heads, local_images, block_images, factor)
            / totals[:, :, None]
        )
        weight_cotangent = jnp.einsum(
            "qhe,khe->qhk", cotangent_heads, value_heads, preferred_element_type=jnp.float32
        )
        score_cotangent = (weights * (weight_cotangent - delta_rows[:, :, None])).astype(
            jnp.bfloat16
        )
        return carried + jnp.einsum(
            "qhk,khe->qhe", score_cotangent, key_heads, preferred_element_type=jnp.float32
        )

    query_sum = lax.fori_loop(
        0, block_count, query_step, jnp.zeros((tokens, HEADS, head_width), jnp.float32)
    )
    all_totals, all_delta = (
        lax.all_gather(totals, "seq", axis=0, tiled=True),
        lax.all_gather(delta_rows, "seq", axis=0, tiled=True),
    )
    local_keys = key_value[:, :inner_width].reshape(tokens, HEADS, head_width)
    local_values = key_value[:, inner_width:].reshape(tokens, HEADS, head_width)
    query_pair = jnp.concatenate([queries, attended_cotangent], axis=1)
    piece_rows = lax.all_gather(query_pair, "seq", axis=0, tiled=True)
    piece_images = lax.all_gather(local_images, "seq", axis=0, tiled=True)
    row_count = piece_rows.shape[0]
    piece_queries = piece_rows[:, :inner_width].reshape(row_count, HEADS, head_width)
    piece_cotangent = piece_rows[:, inner_width:].reshape(row_count, HEADS, head_width)
    weights = (
        exponent(piece_queries, local_keys, piece_images, local_images, factor)
        / all_totals[:, :, None]
    )
    weight_cotangent = jnp.einsum(
        "qhe,khe->qhk", piece_cotangent, local_values, preferred_element_type=jnp.float32
    )
    score_cotangent = (weights * (weight_cotangent - all_delta[:, :, None])).astype(jnp.bfloat16)
    key_part = jnp.einsum(
        "qhk,qhe->khe", score_cotangent, piece_queries, preferred_element_type=jnp.float32
    )
    value_part = jnp.einsum(
        "qhk,qhe->khe",
        weights.astype(jnp.bfloat16),
        piece_cotangent,
        preferred_element_type=jnp.float32,
    )
    key_sum = key_part.reshape(tokens, inner_width)
    value_sum = value_part.reshape(tokens, inner_width)
    input_cotangent = jnp.concatenate(
        [
            (query_sum * factor).reshape(tokens, inner_width).astype(jnp.bfloat16),
            (key_sum * factor).astype(jnp.bfloat16),
            value_sum.astype(jnp.bfloat16),
        ],
        axis=1,
    )
    in_weight_term = lax.dot_general(
        hidden, input_cotangent, contract_rows, preferred_element_type=jnp.float32
    )
    in_summed, out_summed = lax.psum((in_weight_term, out_weight_term), ("grp", "seq"))
    norm_factor = (lax.axis_size("grp") * shard_count * tokens) ** (-0.5)
    hidden_cotangent = lax.dot_general(
        input_cotangent, attention_in, contract_last, preferred_element_type=jnp.float32
    )
    scaled_cot = hidden_cotangent * (1.0 + scale_rows)
    packed_cotangent = upstream + inverse_spread * (
        scaled_cot
        - jnp.mean(scaled_cot, axis=-1, keepdims=True)
        - normed * jnp.mean(scaled_cot * normed, axis=-1, keepdims=True)
    )
    packed_low = packed_cotangent.astype(jnp.bfloat16)
    back_order = jnp.zeros_like(packed_low).at[receive_slot[0, 0]].set(packed_low)
    returned = lax.all_to_all(back_order, "seq", split_axis=0, concat_axis=0, tiled=True)
    owner_gradient = jnp.zeros_like(returned).at[send_rows[0, 0]].set(returned)
    return (
        layer_output[None],
        owner_gradient[None],
        (in_summed * norm_factor).astype(jnp.bfloat16),
        (out_summed * norm_factor).astype(jnp.bfloat16),
    )


def solution(mesh):
    return jax.shard_map(
        shards,
        mesh=mesh,
        in_specs=(
            P("grp", "seq", None),
            P("grp", "seq", None),
            P("grp", "seq", None),
            P("grp", "seq"),
            P("grp", None),
            P("grp", None),
            P(),
            P(),
            P(),
            P(),
            P("grp", "seq", None),
        ),
        out_specs=(P("grp", "seq", None), P("grp", "seq", None), P(), P()),
        check_vma=False,
    )
```

profile of v0, /device:TPU:0, one launch (start us, length us, event | category | flops | bytes accessed | tf_op | source)
XLA Modules:
  0.0 364.4 jit_solution(1085323772350284070)
XLA Ops:
  8.7 2.1 gather_fusion.1
  11.6 6.4 %all-to-all-start = ((bf16[8,16,1152]{2,1,0:T(8,128)(2,1)}), bf16[8,16,1152]{2,1,0:T(8,128)(2,1)S(1)}, u32[]{:S(2)}, u32[]{:S(2)}) async-start(bf16[8,16,1152]{2,1,0:T(8,128)(2,1)} %bitcast.3), calls=%async_computation | async-start | bytes 589824 | tf_op jit(solution)/shard_map/all_to_all | solution.py:48
  18.7 4.5 %fusion.72 = f32[16,3456]{1,0:T(8,128)S(1)} fusion(bf16[1152,3456]{1,0:T(8,128)(2,1)} %param.24, bf16[16,1152]{1,0:T(8,128)(2,1)S(1)} %gather_fusion, pred[16]{0:T(512)(128)(4,1)S(1)} %compare_and_fusion.2), kind=kOutput, calls=%fused_computation.105 | convolution fusion | flops 127531008 | bytes 8220688 | tf_op jit(solution)/shard_map/dot_general | solution.py:53
  24.2 4.2 %all-to-all-done = bf16[8,16,1152]{2,1,0:T(8,128)(2,1)S(1)} async-done(((bf16[8,16,1152]{2,1,0:T(8,128)(2,1)}), bf16[8,16,1152]{2,1,0:T(8,128)(2,1)S(1)}, u32[]{:S(2)}, u32[]{:S(2)}) %all-to-all-start) | async-done | bytes 294944 | tf_op jit(solution)/shard_map/all_to_all | solution.py:48
  30.1 3.4 convolution_convert_fusion
  34.4 1.9 convolution_convert_fusion.1
  37.1 9.8 %all-gather = s32[1,1024]{1,0:T(1,128)S(1)} all-gather(s32[1,128]{1,0:T(1,128)S(1)} %copy-done.19), channel_id=2, replica_groups=mesh['grp'=4,'seq'=8] {'seq'}, dimensions={1}, use_global_device_ids=true | all-gather | bytes 4608 | tf_op jit(solution)/shard_map/all_gather | solution.py:75
  49.5 16.6 %all-gather.4.cloned.1.call-done = bf16[1024,1152]{0,1:T(8,128)(2,1)} async-done(((bf16[128,1152]{0,1:T(8,128)(2,1)}), bf16[1024,1152]{0,1:T(8,128)(2,1)}) %all-gather.4.cloned.1.call-update) | async-done | bytes 2359312 | tf_op jit(solution)/shard_map/all_gather | solution.py:74
  66.1 5.9 %while.30 = (s32[]{:T(128)}, f32[128,8,72]{0,2,1:T(8,128)S(1)}, f32[128,8]{0,1:T(8,128)S(1)}, bf16[1024,1152]{0,1:T(8,128)(2,1)}, s32[1,128]{1,0:T(1,128)S(1)}, ...) while((s32[]{:T(128)}, f32[128,8,72]{0,2,1:T(8,128)S(1)}, ...), condition=%wide.region_4.6_spmd.clone, body=%wide.region_2.5_spmd.clone.sunk | while | flops 154354688 | bytes 8690382 | solution.py:107
  72.0 14.3 %all_gather.19 = f32[1024,8]{0,1:T(8,128)S(1)} all-gather(f32[128,8]{0,1:T(8,128)S(1)} %get-tuple-element.554), channel_id=1, replica_groups=mesh['grp'=4,'seq'=8] {'seq'}, dimensions={0}, use_global_device_ids=true | all-gather | bytes 36864 | tf_op jit(solution)/shard_map/all_gather | solution.py:147
  86.4 14.5 %all_gather.20 = f32[1024,8]{0,1:T(8,128)S(1)} all-gather(f32[128,8]{0,1:T(8,128)S(1)} %get-tuple-element.556), channel_id=1, replica_groups=mesh['grp'=4,'seq'=8] {'seq'}, dimensions={0}, use_global_device_ids=true | all-gather | bytes 36864 | tf_op jit(solution)/shard_map/all_gather | solution.py:148
  100.9 12.1 %while.31 = (s32[]{:T(128)}, f32[128,8,72]{0,2,1:T(8,128)S(1)}, bf16[1024,1152]{0,1:T(8,128)(2,1)}, s32[1,128]{1,0:T(1,128)S(1)}, s32[1024]{0:T(1024)S(1)}, /*in...) while((s32[]{:T(128)}, f32[128,8,72]{0,2,1:T(8,128)S(1)}, ...), condition=%wide.region_7.9_spmd.clone, body=%wide.region_6.8_spmd.clone.sunk | while | flops 229851136 | bytes 9943801 | solution.py:143
  101.1 1.4 fusion.140
  102.5 1.7 fusion.141
  104.2 2.7 fusion.142
  107.2 1.4 fusion.140
  108.5 1.7 fusion.141
  110.3 2.7 fusion.142
  113.1 3.1 fusion.86
  116.3 1.9 fusion.91
  118.2 1.3 fusion.31
  121.4 4.5 %fusion.39 = bf16[8,72,128]{2,1,0:T(8,128)(2,1)} fusion(bf16[1024,8,72]{0,2,1:T(8,128)(2,1)S(1)} %bitcast.192, f32[1024,8,128]{0,2,1:T(8,128)} %copy-done.2, bf16[128,8,72]{0,2,1:T(8,128)(2,1)} %bitcast.205, bf16[1024,8,72]{0,2,1:T(8,128)(2,1)S(1)} %bitcast.190, f32[1024,8]{0,1:T(8,128)S(1)} %all_gather.20), kind=kOutput, calls=%fused_computation.58 | convolution fusion | flops 305283072 | bytes 6881280 | tf_op jit(solution)/shard_map/qhk,qhe->khe/dot_general | solution.py:166
  126.0 5.2 %fusion.63 = f32[1152,1728]{0,1:T(8,128)} fusion(bf16[128,1152]{1,0:T(8,128)(2,1)S(1)} %copy-done.9, bf16[128,576]{0,1:T(8,128)(2,1)S(1)} %bitcast.199, bf16[128,576]{0,1:T(8,128)(2,1)} %bitcast.203, bf16[128,576]{0,1:T(8,128)(2,1)S(1)} %bitcast.201), kind=kOutput, calls=%fused_computation.93 | convolution fusion | flops 510935040 | bytes 8699904 | tf_op jit(solution)/shard_map/dot_general | solution.py:185
  131.2 1.4 copy-done.4
  132.7 3.1 fusion.89
  135.8 2.1 scatter_custom_fusion
  137.9 4.4 %all-to-all-start.1 = ((bf16[8,16,1152]{2,1,0:T(8,128)(2,1)}), bf16[8,16,1152]{2,1,0:T(8,128)(2,1)S(1)}, u32[]{:S(2)}, u32[]{:S(2)}) async-start(bf16[8,16,1152]{2,1,0:T(8,128)(2,1)} %bitcast.31), calls=%async_computation.1 | async-start | bytes 589824 | tf_op jit(solution)/shard_map/all_to_all | solution.py:201
  142.3 2.5 fusion.34
  144.9 10.5 %all-to-all-done.1 = bf16[8,16,1152]{2,1,0:T(8,128)(2,1)S(1)} async-done(((bf16[8,16,1152]{2,1,0:T(8,128)(2,1)}), bf16[8,16,1152]{2,1,0:T(8,128)(2,1)S(1)}, u32[]{:S(2)}, u32[]{:S(2)}) %all-to-all-start.1) | async-done | bytes 294944 | tf_op jit(solution)/shard_map/all_to_all | solution.py:201
  155.4 1.8 scatter_custom_fusion.1
  157.2 193.4 %all-reduce.3.cloned.1.call-done = (f32[1152,1728]{0,1:T(8,128)}, f32[576,1152]{1,0:T(8,128)}) async-done(((f32[1152,1728]{0,1:T(8,128)}, f32[576,1152]{1,0:T(8,128)}), (f32[1152,1728]{0,1:T(8,128)}, f32[576,1152]{1,0:T(8,128)})) %all-reduce.3.cloned.1.call-update) | async-done | bytes 10616848 | tf_op jit(solution)/shard_map/psum | solution.py:188
  350.6 6.0 %multiply_convert_fusion = bf16[1152,1728]{0,1:T(8,128)(2,1)} fusion(f32[1152,1728]{0,1:T(8,128)} %get-tuple-element.384), kind=kLoop, calls=%fused_computation.40 | loop fusion | flops 3981312 | bytes 11943936 | tf_op jit(solution)/shard_map/convert_element_type | solution.py:206
  (106 shorter events, 19.4 us)
Async XLA Ops:
  7.2 11.0 %copy-start = (bf16[1001,1152]{1,0:T(8,128)(2,1)S(1)}, bf16[1001,1152]{1,0:T(8,128)(2,1)}, u32[]{:S(2)}) copy-start(bf16[1001,1152]{1,0:T(8,128)(2,1)} %param.23) | copy-start | bytes 6918916
  7.2 10.9 %copy-start.21 = (s32[1,16]{1,0:T(1,128)S(1)}, s32[1,16]{1,0:T(1,128)}, u32[]{:S(2)}) copy-start(s32[1,16]{1,0:T(1,128)} %param.22) | copy-start | bytes 196
  7.2 10.9 %copy-start.20 = (s32[1,16]{1,0:T(1,128)S(1)}, s32[1,16]{1,0:T(1,128)}, u32[]{:S(2)}) copy-start(s32[1,16]{1,0:T(1,128)} %param.21) | copy-start | bytes 196
  7.2 10.9 %copy-start.22 = (s32[1,1,128]{2,1,0:T(1,128)S(1)}, s32[1,1,128]{2,1,0:T(1,128)}, u32[]{:S(2)}) copy-start(s32[1,1,128]{2,1,0:T(1,128)} %param.19) | copy-start | bytes 1540
  11.6 16.8 %all-to-all-start = ((bf16[8,16,1152]{2,1,0:T(8,128)(2,1)}), bf16[8,16,1152]{2,1,0:T(8,128)(2,1)S(1)}, u32[]{:S(2)}, u32[]{:S(2)}) async-start(bf16[8,16,1152]{2,1,0:T(8,128)(2,1)} %bitcast.3), calls=%async_computation | async-start | bytes 589824 | tf_op jit(solution)/shard_map/all_to_all | solution.py:48
  18.0 48.1 %all-gather.4.cloned.1.call-start = ((), (), s32[]{:S(2)}) async-start(), calls=%async_computation.2 | async-start | bytes 2654208 | tf_op jit(solution)/shard_map/all_gather | solution.py:74
  18.7 4.5 %copy-start.19 = (s32[1,128]{1,0:T(1,128)S(1)}, s32[1,128]{1,0:T(1,128)}, u32[]{:S(2)}) copy-start(s32[1,128]{1,0:T(1,128)} %param.20) | copy-start | bytes 1540
  24.1 10.2 %copy-start.3 = (f32[128,3456]{1,0:T(8,128)}, f32[128,3456]{1,0:T(8,128)S(1)}, u32[]{:S(2)}) copy-start(f32[128,3456]{1,0:T(8,128)S(1)} %fusion.71) | copy-start | bytes 5308420
  30.1 3.5 copy-start.8
  30.1 4.3 %copy-start.5 = (bf16[1,128,1152]{2,1,0:T(8,128)(2,1)S(1)}, bf16[1,128,1152]{2,1,0:T(8,128)(2,1)}, u32[]{:S(2)}) copy-start(bf16[1,128,1152]{2,1,0:T(8,128)(2,1)} %param.27) | copy-start | bytes 884740
  34.3 82.0 %all-gather.6.cloned.1.call-start = ((), (), s32[]{:S(2)}) async-start(), calls=%async_computation.3 | async-start | bytes 2654208 | tf_op jit(solution)/shard_map/all_gather | solution.py:153
  49.4 301.2 %all-reduce.3.cloned.1.call-start = ((), (), s32[]{:S(2)}) async-start(), calls=%async_computation.4 | async-start | bytes 21233664 | tf_op jit(solution)/shard_map/psum | solution.py:188
  66.1 34.8 %copy-start.15 = (f32[128,8,72]{0,2,1:T(8,128)S(1)}, f32[128,8,72]{0,2,1:T(8,128)}, u32[]{:S(2)}) copy-start(f32[128,8,72]{0,2,1:T(8,128)} %custom-call.2) | copy-start | bytes 884740
  86.4 26.7 %copy-start.10 = (bf16[128,8,72]{0,2,1:T(8,128)(2,1)}, bf16[128,8,72]{0,2,1:T(8,128)(2,1)S(1)}, u32[]{:S(2)}) copy-start(bf16[128,8,72]{0,2,1:T(8,128)(2,1)S(1)} %get-tuple-element.387) | copy-start | bytes 442372
  101.1 3.1 copy-start.16
  107.2 3.1 copy-start.16
  113.1 12.9 %copy-start.12 = (bf16[128,8,72]{0,2,1:T(8,128)(2,1)}, bf16[128,8,72]{0,2,1:T(8,128)(2,1)S(1)}, u32[]{:S(2)}) copy-start(bf16[128,8,72]{0,2,1:T(8,128)(2,1)S(1)} %multiply_convert_fusion.2) | copy-start | bytes 442372
  116.2 1.9 copy-start.17
  116.3 1.9 copy-start.18
  119.5 1.9 copy-start.2
  121.4 4.5 %copy-start.9 = (bf16[128,1152]{1,0:T(8,128)(2,1)S(1)}, bf16[128,1152]{1,0:T(8,128)(2,1)}, u32[]{:S(2)}) copy-start(bf16[128,1152]{1,0:T(8,128)(2,1)} %copy-done.8) | copy-start | bytes 884740
  131.2 1.5 copy-start.4
  131.2 1.5 copy-start.13
  131.2 1.5 copy-start.14
  132.7 3.2 copy-start.6
  132.7 9.7 %copy-start.23 = (s32[1,1,128]{2,1,0:T(1,128)S(1)}, s32[1,1,128]{2,1,0:T(1,128)}, u32[]{:S(2)}) copy-start(s32[1,1,128]{2,1,0:T(1,128)} %param.18) | copy-start | bytes 1540
  135.8 6.5 %copy-start.11 = (bf16[128,8,72]{0,2,1:T(8,128)(2,1)S(1)}, bf16[128,8,72]{0,2,1:T(8,128)(2,1)}, u32[]{:S(2)}) copy-start(bf16[128,8,72]{0,2,1:T(8,128)(2,1)} %copy-done.10) | copy-start | bytes 442372
  137.9 17.5 %all-to-all-start.1 = ((bf16[8,16,1152]{2,1,0:T(8,128)(2,1)}), bf16[8,16,1152]{2,1,0:T(8,128)(2,1)S(1)}, u32[]{:S(2)}, u32[]{:S(2)}) async-start(bf16[8,16,1152]{2,1,0:T(8,128)(2,1)} %bitcast.31), calls=%async_computation.1 | async-start | bytes 589824 | tf_op jit(solution)/shard_map/all_to_all | solution.py:201
  350.6 6.0 %copy-start.7 = (f32[576,1152]{1,0:T(8,128)S(1)}, f32[576,1152]{1,0:T(8,128)}, u32[]{:S(2)}) copy-start(f32[576,1152]{1,0:T(8,128)} %get-tuple-element.385) | copy-start | bytes 7962628
  350.6 7.2 %copy-start.1 = (bf16[1001,1152]{1,0:T(8,128)(2,1)S(1)}, bf16[1001,1152]{1,0:T(8,128)(2,1)}, u32[]{:S(2)}) copy-start(bf16[1001,1152]{1,0:T(8,128)(2,1)} %param.23) | copy-start | bytes 6918916
Sparse Core Ops, SparseCore 0:
  34.4 31.6 all-gather.3
  68.3 31.8 all-gather.5
  131.3 219.2 all-reduce.2
where the time goes:
time: 365 us; the launch traced here: 364 us
  waiting for transfers between devices  225 us (62%)
  matrix products  43.1 us (12%)
  blocking collectives  38.6 us (11%)
  local copies, waits for them, and re-layouts  18.2 us (5%)
  other arithmetic  14.5 us (4%)
  between operations  14.1 us (4%)
  starting transfers between devices  10.9 us (3%)
    psum x1, waiting for transfers between devices, shards(): lax.psum((in_weight_term, out_weight_term), ('grp', 'seq'))  193 us
    all_gather x1, waiting for transfers between devices, shards(): lax.all_gather(key_value, 'seq', axis=0, tiled=True)  16.6 us
    all_gather x1, blocking collectives, shards(): lax.all_gather(delta_rows, 'seq', axis=0, tiled=True)  14.5 us
    all_gather x1, blocking collectives, shards(): lax.all_gather(totals, 'seq', axis=0, tiled=True)  14.3 us
    all_to_all x1, waiting for transfers between devices, shards(): lax.all_to_all(back_order, 'seq', split_axis=0, concat_axis=0, tiled=True)  10.5 us
    all_gather x1, blocking collectives, shards(): lax.all_gather(local_images, 'seq', axis=0, tiled=True)  9.77 us
  transfers between devices with their start and end apart: 5, of which 4 were waited for; matrix products, arithmetic and copies ran while one was open for 12% of the time, Pallas kernels for 0%

commit v1 on v0

--- a/solution.py
+++ b/solution.py
@@ -185,7 +185,7 @@
     in_weight_term = lax.dot_general(
         hidden, input_cotangent, contract_rows, preferred_element_type=jnp.float32
     )
-    in_summed, out_summed = lax.psum((in_weight_term, out_weight_term), ("grp", "seq"))
+    in_summed, out_summed = lax.psum(lax.psum((in_weight_term, out_weight_term), "seq"), "grp")
     norm_factor = (lax.axis_size("grp") * shard_count * tokens) ** (-0.5)
     hidden_cotangent = lax.dot_general(
         input_cotangent, attention_in, contract_last, preferred_element_type=jnp.float32

time: 365 us -> 574 us (1.57)
  waiting for transfers between devices: 225 us -> 434 us
    psum x1 -> x2, waiting for transfers between devices: 193 us -> 405 us  [the longest x1 217 us: shards(): lax.psum((in_weight_term, out_weight_term), 'seq')]
  transfers between devices with their start and end apart: 5 -> 6, of which waited for: 4 -> 5; matrix products, arithmetic and copies ran while one was open for 12% -> 7% of each run, Pallas kernels for 0% -> 0%
where the time goes in v1:
time: 574 us; the launch traced here: 573 us
  waiting for transfers between devices  434 us (76%)
  matrix products  43.1 us (8%)
  blocking collectives  38.6 us (7%)
  local copies, waits for them, and re-layouts  18.1 us (3%)
  other arithmetic  14.5 us (3%)
  between operations  14.2 us (2%)
  starting transfers between devices  10.4 us (2%)
    psum x1, waiting for transfers between devices, shards(): lax.psum((in_weight_term, out_weight_term), 'seq')  217 us
    psum x1, waiting for transfers between devices, shards(): lax.psum(lax.psum((in_weight_term, out_weight_term), 'seq'), 'grp')  189 us
    all_gather x1, waiting for transfers between devices, shards(): lax.all_gather(key_value, 'seq', axis=0, tiled=True)  16.6 us
    all_gather x1, blocking collectives, shards(): lax.all_gather(delta_rows, 'seq', axis=0, tiled=True)  14.5 us
    all_gather x1, blocking collectives, shards(): lax.all_gather(totals, 'seq', axis=0, tiled=True)  14.3 us
  transfers between devices with their start and end apart: 6, of which 5 were waited for; matrix products, arithmetic and copies ran while one was open for 7% of the time, Pallas kernels for 0%

profile of v1, /device:TPU:0, one launch (start us, length us, event | category | flops | bytes accessed | tf_op | source)
XLA Modules:
  0.0 573.0 jit_solution(12027214054262582208)
XLA Ops:
  8.7 2.1 gather_fusion.1
  11.6 6.4 %all-to-all-start = ((bf16[8,16,1152]{2,1,0:T(8,128)(2,1)}), bf16[8,16,1152]{2,1,0:T(8,128)(2,1)S(1)}, u32[]{:S(2)}, u32[]{:S(2)}) async-start(bf16[8,16,1152]{2,1,0:T(8,128)(2,1)} %bitcast.3), calls=%async_computation | async-start | bytes 589824 | tf_op jit(solution)/shard_map/all_to_all | solution.py:48
  18.7 4.5 fusion.72
  24.2 4.2 all-to-all-done
  30.1 3.4 convolution_convert_fusion
  34.4 1.9 convolution_convert_fusion.1
  37.1 9.8 %all-gather = s32[1,1024]{1,0:T(1,128)S(1)} all-gather(s32[1,128]{1,0:T(1,128)S(1)} %copy-done.19), channel_id=2, replica_groups=mesh['grp'=4,'seq'=8] {'seq'}, dimensions={1}, use_global_device_ids=true | all-gather | bytes 4608 | tf_op jit(solution)/shard_map/all_gather | solution.py:75
  49.5 16.6 %all-gather.4.cloned.1.call-done = bf16[1024,1152]{0,1:T(8,128)(2,1)} async-done(((bf16[128,1152]{0,1:T(8,128)(2,1)}), bf16[1024,1152]{0,1:T(8,128)(2,1)}) %all-gather.4.cloned.1.call-update) | async-done | bytes 2359312 | tf_op jit(solution)/shard_map/all_gather | solution.py:74
  66.1 5.9 %while.30 = (s32[]{:T(128)}, f32[128,8,72]{0,2,1:T(8,128)S(1)}, f32[128,8]{0,1:T(8,128)S(1)}, bf16[1024,1152]{0,1:T(8,128)(2,1)}, s32[1,128]{1,0:T(1,128)S(1)}, ...) while((s32[]{:T(128)}, f32[128,8,72]{0,2,1:T(8,128)S(1)}, ...), condition=%wide.region_4.6_spmd.clone, body=%wide.region_2.5_spmd.clone.sunk | while | flops 154354688 | bytes 8690382 | solution.py:107
  72.0 14.3 %all_gather.19 = f32[1024,8]{0,1:T(8,128)S(1)} all-gather(f32[128,8]{0,1:T(8,128)S(1)} %get-tuple-element.556), channel_id=1, replica_groups=mesh['grp'=4,'seq'=8] {'seq'}, dimensions={0}, use_global_device_ids=true | all-gather | bytes 36864 | tf_op jit(solution)/shard_map/all_gather | solution.py:147
  86.4 14.5 %all_gather.20 = f32[1024,8]{0,1:T(8,128)S(1)} all-gather(f32[128,8]{0,1:T(8,128)S(1)} %get-tuple-element.558), channel_id=1, replica_groups=mesh['grp'=4,'seq'=8] {'seq'}, dimensions={0}, use_global_device_ids=true | all-gather | bytes 36864 | tf_op jit(solution)/shard_map/all_gather | solution.py:148
  100.9 12.1 %while.31 = (s32[]{:T(128)}, f32[128,8,72]{0,2,1:T(8,128)S(1)}, bf16[1024,1152]{0,1:T(8,128)(2,1)}, s32[1,128]{1,0:T(1,128)S(1)}, s32[1024]{0:T(1024)S(1)}, /*in...) while((s32[]{:T(128)}, f32[128,8,72]{0,2,1:T(8,128)S(1)}, ...), condition=%wide.region_7.9_spmd.clone, body=%wide.region_6.8_spmd.clone.sunk | while | flops 229851136 | bytes 9943801 | solution.py:143
  101.1 1.4 fusion.140
  102.5 1.7 fusion.141
  104.2 2.7 fusion.142
  107.2 1.4 fusion.140
  108.5 1.7 fusion.141
  110.3 2.7 fusion.142
  113.1 3.1 fusion.86
  116.3 1.9 fusion.91
  121.4 4.5 fusion.39
  125.9 5.2 fusion.63
  131.2 216.5 %all-reduce.5.cloned.1.call-done = (f32[1152,1728]{0,1:T(8,128)}, f32[576,1152]{1,0:T(8,128)}) async-done(((f32[1152,1728]{0,1:T(8,128)}, f32[576,1152]{1,0:T(8,128)}), (f32[1152,1728]{0,1:T(8,128)}, f32[576,1152]{1,0:T(8,128)})) %all-reduce.5.cloned.1.call-update) | async-done | bytes 10616848 | tf_op jit(solution)/shard_map/psum | solution.py:188
  347.8 1.4 copy-done.4
  349.3 3.1 fusion.89
  352.4 2.1 scatter_custom_fusion
  354.5 3.8 all-to-all-start.1
  358.4 2.5 fusion.34
  360.9 7.9 %all-to-all-done.1 = bf16[8,16,1152]{2,1,0:T(8,128)(2,1)S(1)} async-done(((bf16[8,16,1152]{2,1,0:T(8,128)(2,1)}), bf16[8,16,1152]{2,1,0:T(8,128)(2,1)S(1)}, u32[]{:S(2)}, u32[]{:S(2)}) %all-to-all-start.1) | async-done | bytes 294944 | tf_op jit(solution)/shard_map/all_to_all | solution.py:201
  368.8 1.8 scatter_custom_fusion.1
  370.6 188.6 %all-reduce.7.cloned.1.call-done = (f32[1152,1728]{0,1:T(8,128)}, f32[576,1152]{1,0:T(8,128)}) async-done(((f32[1152,1728]{0,1:T(8,128)}, f32[576,1152]{1,0:T(8,128)}), (f32[1152,1728]{0,1:T(8,128)}, f32[576,1152]{1,0:T(8,128)})) %all-reduce.7.cloned.1.call-update) | async-done | bytes 10616848 | tf_op jit(solution)/shard_map/psum | solution.py:188
  559.2 6.0 %multiply_convert_fusion = bf16[1152,1728]{0,1:T(8,128)(2,1)} fusion(f32[1152,1728]{0,1:T(8,128)} %get-tuple-element.386), kind=kLoop, calls=%fused_computation.40 | loop fusion | flops 3981312 | bytes 11943936 | tf_op jit(solution)/shard_map/convert_element_type | solution.py:206
  (109 shorter events, 20.8 us)
Async XLA Ops:
  7.2 11.0 %copy-start = (bf16[1001,1152]{1,0:T(8,128)(2,1)S(1)}, bf16[1001,1152]{1,0:T(8,128)(2,1)}, u32[]{:S(2)}) copy-start(bf16[1001,1152]{1,0:T(8,128)(2,1)} %param.23) | copy-start | bytes 6918916
  7.2 10.9 %copy-start.21 = (s32[1,16]{1,0:T(1,128)S(1)}, s32[1,16]{1,0:T(1,128)}, u32[]{:S(2)}) copy-start(s32[1,16]{1,0:T(1,128)} %param.22) | copy-start | bytes 196
  7.2 10.9 %copy-start.20 = (s32[1,16]{1,0:T(1,128)S(1)}, s32[1,16]{1,0:T(1,128)}, u32[]{:S(2)}) copy-start(s32[1,16]{1,0:T(1,128)} %param.21) | copy-start | bytes 196
  7.2 10.9 %copy-start.22 = (s32[1,1,128]{2,1,0:T(1,128)S(1)}, s32[1,1,128]{2,1,0:T(1,128)}, u32[]{:S(2)}) copy-start(s32[1,1,128]{2,1,0:T(1,128)} %param.19) | copy-start | bytes 1540
  11.6 16.8 %all-to-all-start = ((bf16[8,16,1152]{2,1,0:T(8,128)(2,1)}), bf16[8,16,1152]{2,1,0:T(8,128)(2,1)S(1)}, u32[]{:S(2)}, u32[]{:S(2)}) async-start(bf16[8,16,1152]{2,1,0:T(8,128)(2,1)} %bitcast.3), calls=%async_computation | async-start | bytes 589824 | tf_op jit(solution)/shard_map/all_to_all | solution.py:48
  18.0 48.1 %all-gather.4.cloned.1.call-start = ((), (), s32[]{:S(2)}) async-start(), calls=%async_computation.2 | async-start | bytes 2654208 | tf_op jit(solution)/shard_map/all_gather | solution.py:74
  18.7 4.5 copy-start.19
  24.1 10.2 %copy-start.3 = (f32[128,3456]{1,0:T(8,128)}, f32[128,3456]{1,0:T(8,128)S(1)}, u32[]{:S(2)}) copy-start(f32[128,3456]{1,0:T(8,128)S(1)} %fusion.71) | copy-start | bytes 5308420
  30.1 3.5 copy-start.8
  30.1 4.3 copy-start.5
  34.3 82.0 %all-gather.6.cloned.1.call-start = ((), (), s32[]{:S(2)}) async-start(), calls=%async_computation.3 | async-start | bytes 2654208 | tf_op jit(solution)/shard_map/all_gather | solution.py:153
  49.4 298.3 %all-reduce.5.cloned.1.call-start = ((), (), s32[]{:S(2)}) async-start(), calls=%async_computation.4 | async-start | bytes 21233664 | tf_op jit(solution)/shard_map/psum | solution.py:188
  66.1 34.8 %copy-start.15 = (f32[128,8,72]{0,2,1:T(8,128)S(1)}, f32[128,8,72]{0,2,1:T(8,128)}, u32[]{:S(2)}) copy-start(f32[128,8,72]{0,2,1:T(8,128)} %custom-call.2) | copy-start | bytes 884740
  86.4 26.7 %copy-start.10 = (bf16[128,8,72]{0,2,1:T(8,128)(2,1)}, bf16[128,8,72]{0,2,1:T(8,128)(2,1)S(1)}, u32[]{:S(2)}) copy-start(bf16[128,8,72]{0,2,1:T(8,128)(2,1)S(1)} %get-tuple-element.389) | copy-start | bytes 442372
  101.1 3.1 copy-start.16
  107.2 3.1 copy-start.16
  113.1 12.8 %copy-start.12 = (bf16[128,8,72]{0,2,1:T(8,128)(2,1)}, bf16[128,8,72]{0,2,1:T(8,128)(2,1)S(1)}, u32[]{:S(2)}) copy-start(bf16[128,8,72]{0,2,1:T(8,128)(2,1)S(1)} %multiply_convert_fusion.2) | copy-start | bytes 442372
  116.2 1.9 copy-start.17
  116.3 1.9 copy-start.18
  119.5 1.9 copy-start.2
  121.4 4.5 copy-start.9
  131.2 428.0 %all-reduce.7.cloned.1.call-start = ((), (), s32[]{:S(2)}) async-start(), calls=%async_computation.5 | async-start | bytes 21233664 | tf_op jit(solution)/shard_map/psum | solution.py:188
  347.8 1.5 copy-start.4
  347.8 1.5 copy-start.13
  347.8 1.5 copy-start.14
  349.3 3.2 copy-start.6
  349.3 9.1 %copy-start.23 = (s32[1,1,128]{2,1,0:T(1,128)S(1)}, s32[1,1,128]{2,1,0:T(1,128)}, u32[]{:S(2)}) copy-start(s32[1,1,128]{2,1,0:T(1,128)} %param.18) | copy-start | bytes 1540
  352.4 6.0 %copy-start.11 = (bf16[128,8,72]{0,2,1:T(8,128)(2,1)S(1)}, bf16[128,8,72]{0,2,1:T(8,128)(2,1)}, u32[]{:S(2)}) copy-start(bf16[128,8,72]{0,2,1:T(8,128)(2,1)} %copy-done.10) | copy-start | bytes 442372
  354.5 14.3 %all-to-all-start.1 = ((bf16[8,16,1152]{2,1,0:T(8,128)(2,1)}), bf16[8,16,1152]{2,1,0:T(8,128)(2,1)S(1)}, u32[]{:S(2)}, u32[]{:S(2)}) async-start(bf16[8,16,1152]{2,1,0:T(8,128)(2,1)} %bitcast.31), calls=%async_computation.1 | async-start | bytes 589824 | tf_op jit(solution)/shard_map/all_to_all | solution.py:201
  559.2 6.0 %copy-start.7 = (f32[576,1152]{1,0:T(8,128)S(1)}, f32[576,1152]{1,0:T(8,128)}, u32[]{:S(2)}) copy-start(f32[576,1152]{1,0:T(8,128)} %get-tuple-element.387) | copy-start | bytes 7962628
  559.2 7.2 %copy-start.1 = (bf16[1001,1152]{1,0:T(8,128)(2,1)S(1)}, bf16[1001,1152]{1,0:T(8,128)(2,1)}, u32[]{:S(2)}) copy-start(bf16[1001,1152]{1,0:T(8,128)(2,1)} %param.23) | copy-start | bytes 6918916
Sparse Core Ops, SparseCore 0:
  34.4 31.6 all-gather.3
  68.3 31.8 all-gather.5
  131.3 216.4 all-reduce.4
  351.4 207.7 all-reduce.6
